TPU v7x, 256 devices: a whole 4x4x8 slice. The times are simulated.
256 devices in a mesh: seg: 4 (over y), bond: 64 (over z, x, core).
Axes of the slice: x: 4, y: 4, z: 8, core: 2. Of those that a mesh axis runs over, the one named last changes fastest.
Arguments:
- sites: float32 [4, 2, 8192, 8192], P('seg', None, 'bond'), may hold values from -0.6629126 to 0.6629126, as said below
- boundary: float32 [8192], P('bond'), may hold values from -6 to 6
- bits: int32 [32, 4], P(None, 'seg'), may hold values from 0 to 1
- order: int32 [32], replicated, may hold values from 0 to 31, each once
Outputs:
- probs: float32 [32, 4], P(None, 'seg')
Inputs may be any that keep to these rules, and one draw needn't show every extreme that they name: `order`: each slot number appears once. `sites`: real entries.
All inputs are finite; a program needn't handle non-finite values.
Results may differ from a plain program's by a relative error of at most 0.0001.
Values sent between devices are 32-bit elements; how exact they have to be, the bound alone decides.
A program may use at most 64 MiB of HBM per device.

v0:
```python
import jax
import jax.numpy as jnp
from jax import lax
from jax.sharding import PartitionSpec as P

D = 8192
ROWS = 32
MB = 32
EPSILON = 1e-06


def shifted(array, axis, by):
    count = lax.axis_size(axis)
    pairs = [(i, i + by) for i in range(count) if 0 <= i + by < count]
    return lax.ppermute(array, axis, pairs)


def advance(site_piece, env_cols, scale, outcome):
    slots = env_cols.shape[1]
    term = jnp.einsum(
        "slr,lm->rsm",
        site_piece,
        env_cols,
        precision=lax.Precision.HIGHEST,
        preferred_element_type=jnp.float32,
    )
    shard = lax.psum_scatter(
        term.reshape(lax.axis_size("bond") * site_piece.shape[1], 2 * slots),
        "bond",
        scatter_dimension=0,
        tiled=True,
    )
    amps = shard.reshape(shard.shape[0], 2, slots)
    local_sq = jnp.sum(amps * amps, axis=0)
    totals = lax.psum(local_sq, "bond")
    means = totals / (D * scale)[None, :] + EPSILON
    picked = outcome == 1
    chosen = jnp.where(picked[None, :], amps[:, 1, :], amps[:, 0, :])
    weight = jnp.where(picked, means[1], means[0])
    probs = weight / (means[0] + means[1])
    env_next = chosen * lax.rsqrt(scale * weight)[None, :]
    scale_next = jnp.ones_like(scale)
    return (env_next, scale_next, probs)


def on_device(sites, boundary, bits, order):
    group = lax.axis_index("seg")
    sections = lax.axis_size("seg")
    block = MB
    count = ROWS // block
    steps = count + sections - 1
    slot_bits = jnp.take(bits, order, axis=0)
    local_width = sites.shape[2]
    start_env = jnp.broadcast_to(boundary[:, None], (local_width, block))
    unit_scale = jnp.ones((block,), jnp.float32)

    def one_step(step, carry):
        env_in, scale_in, table = carry
        batch = step - group
        valid = jnp.logical_and(batch >= 0, batch < count)
        clipped = jnp.clip(batch, 0, count - 1)
        first = group == 0
        env_cols = jnp.where(first, start_env, env_in)
        scale = jnp.where(first, unit_scale, scale_in)
        env_cols, scale, probs = advance(sites[0], env_cols, scale, slot_bits[:, 0])
        columns = [probs]
        block_probs = jnp.stack(columns, axis=1)
        updated = lax.dynamic_update_slice(table, block_probs, (clipped * block, jnp.int32(0)))
        table = jnp.where(valid, updated, table)
        env_out = shifted(env_cols, "seg", 1)
        return (env_out, scale, table)

    table_init = jnp.zeros((ROWS, sites.shape[0]), jnp.float32)
    env_init = jnp.zeros((local_width, block), jnp.float32)
    final = lax.fori_loop(0, steps, one_step, (env_init, unit_scale, table_init))
    return final[2]


def solution(mesh):
    return jax.shard_map(
        on_device,
        mesh=mesh,
        in_specs=(P("seg", None, "bond", None), P("bond"), P(None, "seg"), P()),
        out_specs=P(None, "seg"),
        check_vma=False,
    )
```

profile of v0, /device:TPU:8, one launch (start us, length us, event | category | flops | bytes accessed | tf_op | source)
XLA Modules:
  0.0 1134.0 jit_solution(4633171038704699626)
XLA Ops:
  6.5 0.0 copy-start
  6.5 0.7 compare_select_fusion
  7.2 0.0 copy-done
  7.2 0.7 gather_fusion
  7.9 0.7 fusion.14
  8.6 1118.4 %while.17 = (s32[]{:T(128)}, f32[128,32]{0,1:T(8,128)S(1)}, f32[32,1]{0,1:T(1,128)S(1)}, s32[32,1]{0,1:T(1,128)S(1)}, pred[]{:T(512)}, /*index=5*/f32[1,2,128,81...) while((s32[]{:T(128)}, f32[128,32]{0,1:T(8,128)S(1)}, f32[32,1]{0,1:T(1,128)S(1)}, ...), condition=%wide.region_4.5_spmd.clone, body=%wide.region_0.4_spmd.clone.sunk | while | flops 805335488 | bytes 17043360 | solution.py:75
  8.6 0.0 reduce-scatter.2.cloned.1.call-start
  8.6 7.7 fusion.23
  16.3 0.0 reduce-scatter.2.cloned.1.call-update
  16.4 144.5 %reduce-scatter.2.cloned.1.call-done = f32[128,64]{0,1:T(8,128)} async-done(((f32[8192,64]{0,1:T(8,128)}), f32[128,64]{0,1:T(8,128)}) %reduce-scatter.2.cloned.1.call-update) | async-done | bytes 32784 | tf_op jit(solution)/shard_map/while/body/eval_jaxpr/reduce_scatter | solution.py:27
  160.9 0.9 multiply_reduce_fusion.2
  161.8 0.1 reduce_sum.19
  161.9 124.0 %psum.14 = f32[2,32]{1,0:T(2,128)S(1)} all-reduce(f32[2,32]{1,0:T(2,128)S(1)} %reduce_sum.19), channel_id=1, replica_groups=mesh['seg'=4,'bond'=64] {'bond'}, use_global_device_ids=true, to_apply=%region_3.3 | all-reduce | flops 64 | bytes 512 | tf_op jit(solution)/shard_map/while/body/eval_jaxpr/psum | solution.py:35
  285.9 0.8 fusion.26
  286.7 3.4 collective-permute-start
  290.2 2.2 collective-permute-done
  292.4 0.0 reduce-scatter.2.cloned.1.call-start
  292.4 7.7 fusion.23
  300.1 0.0 reduce-scatter.2.cloned.1.call-update
  300.1 139.0 %reduce-scatter.2.cloned.1.call-done = f32[128,64]{0,1:T(8,128)} async-done(((f32[8192,64]{0,1:T(8,128)}), f32[128,64]{0,1:T(8,128)}) %reduce-scatter.2.cloned.1.call-update) | async-done | bytes 32784 | tf_op jit(solution)/shard_map/while/body/eval_jaxpr/reduce_scatter | solution.py:27
  439.1 0.9 multiply_reduce_fusion.2
  440.0 0.1 reduce_sum.19
  440.0 124.0 %psum.14 = f32[2,32]{1,0:T(2,128)S(1)} all-reduce(f32[2,32]{1,0:T(2,128)S(1)} %reduce_sum.19), channel_id=1, replica_groups=mesh['seg'=4,'bond'=64] {'bond'}, use_global_device_ids=true, to_apply=%region_3.3 | all-reduce | flops 64 | bytes 512 | tf_op jit(solution)/shard_map/while/body/eval_jaxpr/psum | solution.py:35
  564.1 0.8 fusion.26
  564.9 3.4 collective-permute-start
  568.4 2.2 collective-permute-done
  570.5 0.0 reduce-scatter.2.cloned.1.call-start
  570.6 7.7 fusion.23
  578.2 0.0 reduce-scatter.2.cloned.1.call-update
  578.3 139.0 %reduce-scatter.2.cloned.1.call-done = f32[128,64]{0,1:T(8,128)} async-done(((f32[8192,64]{0,1:T(8,128)}), f32[128,64]{0,1:T(8,128)}) %reduce-scatter.2.cloned.1.call-update) | async-done | bytes 32784 | tf_op jit(solution)/shard_map/while/body/eval_jaxpr/reduce_scatter | solution.py:27
  717.3 0.9 multiply_reduce_fusion.2
  718.2 0.1 reduce_sum.19
  718.3 124.0 %psum.14 = f32[2,32]{1,0:T(2,128)S(1)} all-reduce(f32[2,32]{1,0:T(2,128)S(1)} %reduce_sum.19), channel_id=1, replica_groups=mesh['seg'=4,'bond'=64] {'bond'}, use_global_device_ids=true, to_apply=%region_3.3 | all-reduce | flops 64 | bytes 512 | tf_op jit(solution)/shard_map/while/body/eval_jaxpr/psum | solution.py:35
  842.3 0.8 fusion.26
  843.1 3.4 collective-permute-start
  846.6 2.2 collective-permute-done
  848.8 0.0 reduce-scatter.2.cloned.1.call-start
  848.8 7.7 fusion.23
  856.5 0.0 reduce-scatter.2.cloned.1.call-update
  856.5 139.0 %reduce-scatter.2.cloned.1.call-done = f32[128,64]{0,1:T(8,128)} async-done(((f32[8192,64]{0,1:T(8,128)}), f32[128,64]{0,1:T(8,128)}) %reduce-scatter.2.cloned.1.call-update) | async-done | bytes 32784 | tf_op jit(solution)/shard_map/while/body/eval_jaxpr/reduce_scatter | solution.py:27
  995.5 0.9 multiply_reduce_fusion.2
  996.4 0.1 reduce_sum.19
  996.5 124.0 %psum.14 = f32[2,32]{1,0:T(2,128)S(1)} all-reduce(f32[2,32]{1,0:T(2,128)S(1)} %reduce_sum.19), channel_id=1, replica_groups=mesh['seg'=4,'bond'=64] {'bond'}, use_global_device_ids=true, to_apply=%region_3.3 | all-reduce | flops 64 | bytes 512 | tf_op jit(solution)/shard_map/while/body/eval_jaxpr/psum | solution.py:35
  1120.6 0.8 fusion.26
  1121.4 3.4 collective-permute-start
  1124.8 2.2 collective-permute-done
  1127.0 0.0 copy-start.1
  1127.0 0.5 copy-done.1
  (19 shorter events, 0.2 us)
Async XLA Ops:
  6.5 0.7 copy-start
  8.6 152.3 %reduce-scatter.2.cloned.1.call-start = ((), (), s32[]{:S(2)}) async-start(), calls=%async_computation.1 | async-start | bytes 2129920 | tf_op jit(solution)/shard_map/while/body/eval_jaxpr/reduce_scatter | solution.py:27
  286.7 5.6 collective-permute-start
  292.4 146.7 %reduce-scatter.2.cloned.1.call-start = ((), (), s32[]{:S(2)}) async-start(), calls=%async_computation.1 | async-start | bytes 2129920 | tf_op jit(solution)/shard_map/while/body/eval_jaxpr/reduce_scatter | solution.py:27
  564.9 5.6 collective-permute-start
  570.5 146.8 %reduce-scatter.2.cloned.1.call-start = ((), (), s32[]{:S(2)}) async-start(), calls=%async_computation.1 | async-start | bytes 2129920 | tf_op jit(solution)/shard_map/while/body/eval_jaxpr/reduce_scatter | solution.py:27
  843.1 5.6 collective-permute-start
  848.8 146.8 %reduce-scatter.2.cloned.1.call-start = ((), (), s32[]{:S(2)}) async-start(), calls=%async_computation.1 | async-start | bytes 2129920 | tf_op jit(solution)/shard_map/while/body/eval_jaxpr/reduce_scatter | solution.py:27
  1121.4 5.6 collective-permute-start
  1127.0 0.5 copy-start.1
Sparse Core Ops, SparseCore 0:
  16.5 144.3 reduce-scatter.1
  300.2 138.8 reduce-scatter.1
  578.4 138.8 reduce-scatter.1
  856.6 138.8 reduce-scatter.1
where the time goes:
time: 1140 us; the launch traced here: 1130 us
  waiting for transfers between devices  570 us (50%)
  blocking collectives  496 us (44%)
  matrix products  30.8 us (3%)
  starting transfers between devices  13.7 us (1%)
  between operations  13.1 us (1%)
    reduce_scatter x4, waiting for transfers between devices, advance(): lax.psum_scatter(term.reshape(lax.axis_size('bond') * site_piece.shape[1]...  562 us
    psum x4, blocking collectives, advance(): totals = lax.psum(local_sq, 'bond')  496 us
    dot_general x4, matrix products, advance(): jnp.einsum('slr,lm->rsm', site_piece, env_cols, precision=lax.Precision.H...  30.8 us
  transfers between devices with their start and end apart: 8, of which 8 were waited for; matrix products, arithmetic and copies ran while one was open for 0% of the time, Pallas kernels for 0%

commit v1 on v0

--- a/solution.py
+++ b/solution.py
@@ -32,7 +32,7 @@
     )
     amps = shard.reshape(shard.shape[0], 2, slots)
     local_sq = jnp.sum(amps * amps, axis=0)
-    totals = lax.psum(local_sq, "bond")
+    totals = jnp.sum(lax.all_gather(local_sq, "bond"), axis=0)
     means = totals / (D * scale)[None, :] + EPSILON
     picked = outcome == 1
     chosen = jnp.where(picked[None, :], amps[:, 1, :], amps[:, 0, :])

time: 1140 us -> 811 us (0.71)
  blocking collectives: 496 us -> 170 us
    psum x4 -> x0, blocking collectives: 496 us -> none  [advance(): totals = lax.psum(local_sq, 'bond')]
    all_gather x0 -> x4, blocking collectives: none -> 170 us  [advance(): totals = jnp.sum(lax.all_gather(local_sq, 'bond'), axis=0)]
where the time goes in v1:
time: 811 us; the launch traced here: 810 us
  waiting for transfers between devices  573 us (71%)
  blocking collectives  170 us (21%)
  matrix products  30.8 us (4%)
  starting transfers between devices  13.6 us (2%)
  between operations  13.1 us (2%)
  other arithmetic  8.49 us (1%)
    reduce_scatter x4, waiting for transfers between devices, advance(): lax.psum_scatter(term.reshape(lax.axis_size('bond') * site_piece.shape[1]...  564 us
    all_gather x4, blocking collectives, advance(): totals = jnp.sum(lax.all_gather(local_sq, 'bond'), axis=0)  170 us
    dot_general x4, matrix products, advance(): jnp.einsum('slr,lm->rsm', site_piece, env_cols, precision=lax.Precision.H...  30.8 us
  transfers between devices with their start and end apart: 8, of which 8 were waited for; matrix products, arithmetic and copies ran while one was open for 0% of the time, Pallas kernels for 0%

profile of v1, /device:TPU:8, one launch (start us, length us, event | category | flops | bytes accessed | tf_op | source)
XLA Modules:
  0.0 810.3 jit_solution(9580434429081330187)
XLA Ops:
  6.5 0.0 copy-start
  6.5 0.7 compare_select_fusion
  7.2 0.0 copy-done
  7.2 0.7 gather_fusion
  7.9 0.7 fusion.14
  8.6 794.6 %while.17 = (s32[]{:T(128)}, f32[128,32]{0,1:T(8,128)S(1)}, f32[32,1]{0,1:T(1,128)S(1)}, s32[32,1]{0,1:T(1,128)S(1)}, pred[]{:T(512)}, /*index=5*/f32[1,2,128,81...) while((s32[]{:T(128)}, f32[128,32]{0,1:T(8,128)S(1)}, ...), condition=%wide.region_4.5_spmd.clone, body=%wide.region_0.4_spmd.clone.sunk | while | flops 805339456 | bytes 17076140 | solution.py:75
  8.6 0.0 reduce-scatter.2.cloned.1.call-start
  8.6 7.7 fusion.23
  16.3 0.0 reduce-scatter.2.cloned.1.call-update
  16.4 144.5 %reduce-scatter.2.cloned.1.call-done = f32[128,64]{0,1:T(8,128)} async-done(((f32[8192,64]{0,1:T(8,128)}), f32[128,64]{0,1:T(8,128)}) %reduce-scatter.2.cloned.1.call-update) | async-done | bytes 32784 | tf_op jit(solution)/shard_map/while/body/eval_jaxpr/reduce_scatter | solution.py:27
  160.9 0.9 multiply_reduce_fusion.2
  161.8 0.1 all_gather.20
  161.9 42.4 %all_gather.21 = f32[64,2,32]{2,1,0:T(2,128)S(1)} all-gather(f32[1,2,32]{2,1,0:T(2,128)S(1)} %all_gather.20), channel_id=1, replica_groups=mesh['seg'=4,'bond'=64] {'bond'}, dimensions={0}, use_global_device_ids=true | all-gather | bytes 16640 | tf_op jit(solution)/shard_map/while/body/eval_jaxpr/all_gather | solution.py:35
  204.3 0.1 reduce_sum.31
  204.4 0.8 fusion.26
  205.2 3.4 collective-permute-start
  208.6 2.2 collective-permute-done
  210.8 7.7 fusion.23
  218.5 0.0 reduce-scatter.2.cloned.1.call-update
  218.6 139.8 %reduce-scatter.2.cloned.1.call-done = f32[128,64]{0,1:T(8,128)} async-done(((f32[8192,64]{0,1:T(8,128)}), f32[128,64]{0,1:T(8,128)}) %reduce-scatter.2.cloned.1.call-update) | async-done | bytes 32784 | tf_op jit(solution)/shard_map/while/body/eval_jaxpr/reduce_scatter | solution.py:27
  358.3 0.9 multiply_reduce_fusion.2
  359.2 0.1 all_gather.20
  359.3 42.4 %all_gather.21 = f32[64,2,32]{2,1,0:T(2,128)S(1)} all-gather(f32[1,2,32]{2,1,0:T(2,128)S(1)} %all_gather.20), channel_id=1, replica_groups=mesh['seg'=4,'bond'=64] {'bond'}, dimensions={0}, use_global_device_ids=true | all-gather | bytes 16640 | tf_op jit(solution)/shard_map/while/body/eval_jaxpr/all_gather | solution.py:35
  401.7 0.1 reduce_sum.31
  401.8 0.8 fusion.26
  402.6 3.4 collective-permute-start
  406.0 2.2 collective-permute-done
  408.2 7.7 fusion.23
  415.9 0.0 reduce-scatter.2.cloned.1.call-update
  416.0 139.9 %reduce-scatter.2.cloned.1.call-done = f32[128,64]{0,1:T(8,128)} async-done(((f32[8192,64]{0,1:T(8,128)}), f32[128,64]{0,1:T(8,128)}) %reduce-scatter.2.cloned.1.call-update) | async-done | bytes 32784 | tf_op jit(solution)/shard_map/while/body/eval_jaxpr/reduce_scatter | solution.py:27
  555.9 0.9 multiply_reduce_fusion.2
  556.7 0.1 all_gather.20
  556.8 42.4 %all_gather.21 = f32[64,2,32]{2,1,0:T(2,128)S(1)} all-gather(f32[1,2,32]{2,1,0:T(2,128)S(1)} %all_gather.20), channel_id=1, replica_groups=mesh['seg'=4,'bond'=64] {'bond'}, dimensions={0}, use_global_device_ids=true | all-gather | bytes 16640 | tf_op jit(solution)/shard_map/while/body/eval_jaxpr/all_gather | solution.py:35
  599.2 0.1 reduce_sum.31
  599.3 0.8 fusion.26
  600.1 3.4 collective-permute-start
  603.5 2.2 collective-permute-done
  605.8 7.7 fusion.23
  613.4 0.0 reduce-scatter.2.cloned.1.call-update
  613.5 139.8 %reduce-scatter.2.cloned.1.call-done = f32[128,64]{0,1:T(8,128)} async-done(((f32[8192,64]{0,1:T(8,128)}), f32[128,64]{0,1:T(8,128)}) %reduce-scatter.2.cloned.1.call-update) | async-done | bytes 32784 | tf_op jit(solution)/shard_map/while/body/eval_jaxpr/reduce_scatter | solution.py:27
  753.3 0.9 multiply_reduce_fusion.2
  754.2 0.1 all_gather.20
  754.3 42.4 %all_gather.21 = f32[64,2,32]{2,1,0:T(2,128)S(1)} all-gather(f32[1,2,32]{2,1,0:T(2,128)S(1)} %all_gather.20), channel_id=1, replica_groups=mesh['seg'=4,'bond'=64] {'bond'}, dimensions={0}, use_global_device_ids=true | all-gather | bytes 16640 | tf_op jit(solution)/shard_map/while/body/eval_jaxpr/all_gather | solution.py:35
  796.7 0.1 reduce_sum.31
  796.8 0.8 fusion.26
  797.6 3.4 collective-permute-start
  801.0 2.2 collective-permute-done
  803.2 0.5 copy-done.1
  (23 shorter events, 0.2 us)
Async XLA Ops:
  6.5 0.7 copy-start
  8.6 152.3 %reduce-scatter.2.cloned.1.call-start = ((), (), s32[]{:S(2)}) async-start(), calls=%async_computation.1 | async-start | bytes 2129920 | tf_op jit(solution)/shard_map/while/body/eval_jaxpr/reduce_scatter | solution.py:27
  205.2 5.6 collective-permute-start
  210.8 147.5 %reduce-scatter.2.cloned.1.call-start = ((), (), s32[]{:S(2)}) async-start(), calls=%async_computation.1 | async-start | bytes 2129920 | tf_op jit(solution)/shard_map/while/body/eval_jaxpr/reduce_scatter | solution.py:27
  402.6 5.6 collective-permute-start
  408.2 147.6 %reduce-scatter.2.cloned.1.call-start = ((), (), s32[]{:S(2)}) async-start(), calls=%async_computation.1 | async-start | bytes 2129920 | tf_op jit(solution)/shard_map/while/body/eval_jaxpr/reduce_scatter | solution.py:27
  600.1 5.6 collective-permute-start
  605.7 147.6 %reduce-scatter.2.cloned.1.call-start = ((), (), s32[]{:S(2)}) async-start(), calls=%async_computation.1 | async-start | bytes 2129920 | tf_op jit(solution)/shard_map/while/body/eval_jaxpr/reduce_scatter | solution.py:27
  797.6 5.6 collective-permute-start
  803.2 0.5 copy-start.1
Sparse Core Ops, SparseCore 0:
  16.5 144.3 reduce-scatter.1
  218.7 139.6 reduce-scatter.1
  416.1 139.7 reduce-scatter.1
  613.6 139.6 reduce-scatter.1
